TPU v7x, 32 devices: a whole 2x2x4 slice. The times are simulated.
32 devices in a mesh: row: 16 (over z, y, x), rep: 2 (over core).
Axes of the slice: x: 2, y: 2, z: 4, core: 2. Of those that a mesh axis runs over, the one named last changes fastest.
Arguments:
- node_feats: bfloat16 [4096, 256], P(('row', 'rep')), may hold values from -6 to 6
- edge_feats: bfloat16 [32768, 256], P(('row', 'rep')), may hold values from -6 to 6
- senders: int32 [32768], P(('row', 'rep')), may hold values from 0 to 4095, as said below
- receivers: int32 [32768], P(('row', 'rep')), may hold values from 0 to 4095, as said below
- edge_count: int32 [32], P(('row', 'rep')), may hold values from 512 to 1024, as said below
- w_edge_in: bfloat16 [768, 256], replicated, may hold values from -0.21875 to 0.21875
- w_edge_out: bfloat16 [256, 256], replicated, may hold values from -0.375 to 0.375
- gain_edge: float32 [256], replicated, may hold values from 0.5 to 2
- w_node_in: bfloat16 [512, 256], replicated, may hold values from -0.25 to 0.25
- w_node_out: bfloat16 [256, 256], replicated, may hold values from -0.375 to 0.375
- gain_node: float32 [256], replicated, may hold values from 0.5 to 2
- d_nodes_out: bfloat16 [4096, 256], P(('row', 'rep')), may hold values from -6 to 6
- d_edges_out: bfloat16 [32768, 256], P(('row', 'rep')), may hold values from -6 to 6
Outputs:
- nodes_out: bfloat16 [4096, 256], P(('row', 'rep'))
- edges_out: bfloat16 [32768, 256], P(('row', 'rep'))
- d_nodes: bfloat16 [4096, 256], P(('row', 'rep'))
- d_edges: bfloat16 [32768, 256], P(('row', 'rep'))
- d_w_edge_in: bfloat16 [768, 256], replicated
- d_w_edge_out: bfloat16 [256, 256], replicated
- d_gain_edge: float32 [256], replicated
- d_w_node_in: bfloat16 [512, 256], replicated
- d_w_node_out: bfloat16 [256, 256], replicated
- d_gain_node: float32 [256], replicated
Inputs may be any that keep to these rules, and one draw needn't show every extreme that they name: `receivers`: edge i's receiver lies in nodes g * 256 to (g + 1) * 256 - 1 with g = i // 2048. `senders`: an edge's sender differs from its receiver by at most 128; in every aligned block of 1024 edge slots some edge reaches 128. The first edge_count[k] slots of the k-th aligned block of 1024 slots are live; some block is full.
All inputs are finite; a program needn't handle non-finite values.
Results may differ from a plain program's by a relative error of at most 0.013.
Values may be sent and summed in bfloat16 or wider, within the bound.
A program may use at most 64 MiB of HBM per device.

v0:
```python
import jax
import jax.numpy as jnp
from jax import lax
from jax.sharding import PartitionSpec as P


def padded(x, sides, width):
    for axis, dim in sides:
        devices, length = (lax.axis_size(axis), x.shape[dim])
        up = [(i, (i + 1) % devices) for i in range(devices - 1)]
        down = [(j, i) for i, j in up]
        last = lax.slice_in_dim(x, length - width, length, axis=dim)
        first = lax.slice_in_dim(x, 0, width, axis=dim)
        before = lax.ppermute(last, axis, up)
        after = lax.ppermute(first, axis, down)
        x = jnp.concatenate([before, x, after], axis=dim)
    return x


def from_behind(value, axis, steps):
    count = lax.axis_size(axis)
    first, last = (max(0, -steps), min(count, count - steps))
    return lax.ppermute(value, axis, [(source, source + steps) for source in range(first, last)])


def silu_slope(pre):
    sigmoid = jax.nn.sigmoid(pre)
    return sigmoid * (1.0 + pre * (1.0 - sigmoid))


def layer_norm(values):
    centred = values - jnp.mean(values, axis=-1, keepdims=True)
    inv_scale = lax.rsqrt(jnp.mean(centred * centred, axis=-1, keepdims=True) + 1e-05)
    return (centred * inv_scale, inv_scale)


def norm_back(upstream, normed, inv_scale):
    return inv_scale * (
        upstream
        - jnp.mean(upstream, axis=-1, keepdims=True)
        - normed * jnp.mean(upstream * normed, axis=-1, keepdims=True)
    )


def contract_rows(left, right):
    return lax.dot_general(
        left, right, (((0,), (0,)), ((), ())), preferred_element_type=jnp.float32
    )


def times_transpose(left, right):
    return lax.dot_general(
        left, right, (((1,), (1,)), ((), ())), preferred_element_type=jnp.float32
    )


def local(
    node_feats,
    edge_feats,
    senders,
    receivers,
    edge_count,
    w_edge_in,
    w_edge_out,
    gain_edge,
    w_node_in,
    w_node_out,
    gain_node,
    d_nodes_out,
    d_edges_out,
):
    width = node_feats.shape[1]
    edge_rows = edge_feats.shape[0]
    grouped = lax.all_gather(node_feats, "rep", axis=0, tiled=True)
    group_rows = grouped.shape[0]
    rim_rows = group_rows // 2
    extended = padded(grouped, (("row", 0),), rim_rows)
    group_start = lax.axis_index("row") * group_rows
    recv_local = receivers - group_start
    send_local = senders - group_start + rim_rows
    slots = jnp.arange(edge_rows, dtype=jnp.int32)
    live_mask = (slots < edge_count[0]).astype(jnp.float32)[:, None]
    edge_input = jnp.concatenate(
        [edge_feats, jnp.take(extended, send_local, axis=0), jnp.take(grouped, recv_local, axis=0)],
        axis=1,
    )
    edge_pre = jnp.dot(edge_input, w_edge_in, preferred_element_type=jnp.float32)
    edge_act = jax.nn.silu(edge_pre).astype(jnp.bfloat16)
    edge_mix = jnp.dot(edge_act, w_edge_out, preferred_element_type=jnp.float32)
    edge_norm, edge_scale = layer_norm(edge_mix)
    message = live_mask * edge_norm * gain_edge
    edges_out = (edge_feats.astype(jnp.float32) + message).astype(jnp.bfloat16)
    message_b = message.astype(jnp.bfloat16)
    recv_table = (
        lax.broadcasted_iota(jnp.int32, (group_rows, edge_rows), 0) == recv_local[None, :]
    ).astype(jnp.bfloat16)
    partial_sums = jnp.dot(recv_table, message_b, preferred_element_type=jnp.float32)
    aggregate = lax.psum_scatter(partial_sums, "rep", scatter_dimension=0, tiled=True)
    node_input = jnp.concatenate([node_feats, aggregate.astype(jnp.bfloat16)], axis=1)
    node_pre = jnp.dot(node_input, w_node_in, preferred_element_type=jnp.float32)
    node_act = jax.nn.silu(node_pre).astype(jnp.bfloat16)
    node_mix = jnp.dot(node_act, w_node_out, preferred_element_type=jnp.float32)
    node_norm, node_scale = layer_norm(node_mix)
    nodes_out = (node_feats.astype(jnp.float32) + node_norm * gain_node).astype(jnp.bfloat16)
    grad_nodes = d_nodes_out.astype(jnp.float32)
    d_gain_node = jnp.sum(grad_nodes * node_norm, axis=0)
    d_node_mix = norm_back(grad_nodes * gain_node, node_norm, node_scale).astype(jnp.bfloat16)
    d_w_node_out = contract_rows(node_act, d_node_mix)
    d_node_pre = (times_transpose(d_node_mix, w_node_out) * silu_slope(node_pre)).astype(
        jnp.bfloat16
    )
    d_w_node_in = contract_rows(node_input, d_node_pre)
    d_node_input = times_transpose(d_node_pre, w_node_in)
    d_aggregate = d_node_input[:, width:].astype(jnp.bfloat16)
    d_direct = grad_nodes + d_node_input[:, :width]
    group_grad = lax.all_gather(d_aggregate, "rep", axis=0, tiled=True)
    d_message = live_mask * (
        d_edges_out.astype(jnp.float32)
        + jnp.take(group_grad, recv_local, axis=0).astype(jnp.float32)
    )
    d_gain_edge = jnp.sum(d_message * edge_norm, axis=0)
    d_edge_mix = norm_back(d_message * gain_edge, edge_norm, edge_scale).astype(jnp.bfloat16)
    d_w_edge_out = contract_rows(edge_act, d_edge_mix)
    d_edge_pre = (times_transpose(d_edge_mix, w_edge_out) * silu_slope(edge_pre)).astype(
        jnp.bfloat16
    )
    d_w_edge_in = contract_rows(edge_input, d_edge_pre)
    d_edge_input = times_transpose(d_edge_pre, w_edge_in)
    d_edges = (d_edges_out.astype(jnp.float32) + d_edge_input[:, :width]).astype(jnp.bfloat16)
    d_sender = d_edge_input[:, width : 2 * width].astype(jnp.bfloat16)
    d_receiver = d_edge_input[:, 2 * width :].astype(jnp.bfloat16)
    send_table = (
        lax.broadcasted_iota(jnp.int32, (group_rows + 2 * rim_rows, edge_rows), 0)
        == send_local[None, :]
    ).astype(jnp.bfloat16)
    send_sums = jnp.dot(send_table, d_sender, preferred_element_type=jnp.float32)
    recv_sums = jnp.dot(recv_table, d_receiver, preferred_element_type=jnp.float32)
    from_next = from_behind(send_sums[:rim_rows].astype(jnp.bfloat16), "row", -1).astype(
        jnp.float32
    )
    from_prev = from_behind(
        send_sums[group_rows + rim_rows :].astype(jnp.bfloat16), "row", 1
    ).astype(jnp.float32)
    inner = send_sums[rim_rows : rim_rows + group_rows]
    inner = jnp.concatenate([inner[:rim_rows] + from_prev, inner[rim_rows:] + from_next], axis=0)
    edge_terms = lax.psum_scatter(
        inner.astype(jnp.bfloat16), "rep", scatter_dimension=0, tiled=True
    ).astype(jnp.float32) + lax.psum_scatter(
        recv_sums.astype(jnp.bfloat16), "rep", scatter_dimension=0, tiled=True
    ).astype(
        jnp.float32
    )
    d_nodes = (d_direct + edge_terms).astype(jnp.bfloat16)
    summed = lax.psum(
        (d_w_edge_in, d_w_edge_out, d_gain_edge, d_w_node_in, d_w_node_out, d_gain_node),
        ("row", "rep"),
    )
    return (
        nodes_out,
        edges_out,
        d_nodes,
        d_edges,
        summed[0].astype(jnp.bfloat16),
        summed[1].astype(jnp.bfloat16),
        summed[2],
        summed[3].astype(jnp.bfloat16),
        summed[4].astype(jnp.bfloat16),
        summed[5],
    )


def solution(mesh):
    return jax.shard_map(
        local,
        mesh=mesh,
        in_specs=(
            P(("row", "rep"), None),
            P(("row", "rep"), None),
            P(("row", "rep")),
            P(("row", "rep")),
            P(("row", "rep")),
            P(),
            P(),
            P(),
            P(),
            P(),
            P(),
            P(("row", "rep"), None),
            P(("row", "rep"), None),
        ),
        out_specs=(
            P(("row", "rep"), None),
            P(("row", "rep"), None),
            P(("row", "rep"), None),
            P(("row", "rep"), None),
            P(),
            P(),
            P(),
            P(),
            P(),
            P(),
        ),
        check_vma=False,
    )
```

profile of v0, /device:TPU:0, one launch (start us, length us, event | category | flops | bytes accessed | tf_op | source)
XLA Modules:
  0.0 151.7 jit_solution(1003866890800980398)
XLA Ops:
  7.2 0.0 copy-start
  7.2 0.0 reduce-scatter.4.cloned.1.call-start
  7.2 2.4 %all_gather.6 = bf16[256,256]{1,0:T(8,128)(2,1)S(1)} all-gather(bf16[128,256]{1,0:T(8,128)(2,1)} %param.15), channel_id=1, replica_groups=mesh['row'=16,'rep'=2] {'rep'}, dimensions={0}, use_global_device_ids=true | all-gather | bytes 196608 | tf_op jit(solution)/shard_map/all_gather | solution.py:74
  9.6 4.7 %collective-permute-start = (bf16[128,256]{1,0:T(8,128)(2,1)S(1)}, bf16[128,256]{1,0:T(8,128)(2,1)S(1)}, u32[]{:S(2)}, u32[]{:S(2)}) collective-permute-start(bf16[128,256]{1,0:T(8,128)(2,1)S(1)} %get-tuple-element.42), channel_id=1, source_target_pairs={{0,2},{2,4},{4,6},{6,8},{8,10},{10,12},{12,14},{14,16},{16,18},{18... | collective-permute-start | bytes 196616 | tf_op jit(solution)/shard_map/ppermute | solution.py:14
  14.4 1.3 collective-permute-start.1
  15.7 0.7 compare_and_fusion.1
  16.4 1.3 subtract_add_fusion
  18.3 0.7 compare_and_fusion
  19.0 3.9 %gather_fusion.1 = bf16[1024,256]{1,0:T(8,128)(2,1)S(1)} fusion(bf16[256,256]{1,0:T(8,128)(2,1)S(1)} %all_gather.6, s32[1024]{0:T(1024)S(1)} %fusion.36), kind=kCustom, calls=%fused_computation.clone | custom fusion | bytes 1052672 | tf_op jit(solution)/shard_map/jit(_take)/gather | solution.py:84
  23.0 0.2 broadcast_select_fusion
  23.3 0.0 copy-start.17
  23.3 3.9 %gather_fusion = bf16[1024,256]{1,0:T(8,128)(2,1)S(1)} fusion(bf16[512,256]{1,0:T(8,128)(2,1)S(1)} %pad_maximum_fusion.3, s32[1024]{0:T(1024)S(1)} %get-tuple-element.45), kind=kCustom, calls=%fused_computation.2 | custom fusion | bytes 1052672 | tf_op jit(solution)/shard_map/jit(_take)/gather | solution.py:84
  27.2 0.2 broadcast_select_fusion.1
  27.5 0.0 copy-start.24
  27.5 1.6 %multiply_convert_fusion.1 = (bf16[1024,256]{1,0:T(8,128)(2,1)S(1)}, f32[1024,256]{1,0:T(8,128)}) fusion(bf16[768,256]{1,0:T(8,128)(2,1)S(1)} %copy-done, bf16[1024,256]{1,0:T(8,128)(2,1)S(1)} %broadcast_select_fusion, bf16[1024,256]{1,0:T(8,128)(2,1)S(1)} %broadcast_select_fusion.1, bf16[1024,256]{1,0:T(8,128)(2,1)S(1)} %copy-done.17), kind=kOutput, calls=%fused_computation.22 | convolution fusion | flops 408682496 | bytes 3538944 | tf_op jit(solution)/shard_map/dot_general | solution.py:87
  29.1 0.4 fusion.47
  29.5 0.1 multiply_reduce_fusion.2
  29.6 0.1 copy-done.33
  29.8 1.2 fusion.6
  30.9 0.0 reduce-scatter.4.cloned.1.call-update
  31.0 0.0 reduce-scatter.8.cloned.1.call-start
  31.0 1.0 copy.23
  32.0 0.2 copy.24
  32.3 9.0 %reduce-scatter.4.cloned.1.call-done = f32[128,256]{1,0:T(8,128)} async-done(((f32[256,256]{1,0:T(8,128)}), f32[128,256]{1,0:T(8,128)}) %reduce-scatter.4.cloned.1.call-update) | async-done | bytes 131088 | tf_op jit(solution)/shard_map/reduce_scatter | solution.py:98
  41.3 0.9 convert_element_type.98
  42.2 0.2 fusion.34
  42.4 1.2 fusion.48
  43.6 0.2 multiply_reduce_fusion.3
  43.8 1.3 fusion.30
  45.1 0.3 fusion.2
  45.4 1.0 fusion.41
  46.4 0.2 fusion.51
  46.6 0.7 copy-done.7
  47.3 1.9 %all_gather.7 = bf16[256,256]{1,0:T(8,128)(2,1)S(1)} all-gather(bf16[128,256]{1,0:T(8,128)(2,1)S(1)} %slice.81), channel_id=1, replica_groups=mesh['row'=16,'rep'=2] {'rep'}, dimensions={0}, use_global_device_ids=true | all-gather | bytes 196608 | tf_op jit(solution)/shard_map/all_gather | solution.py:116
  49.2 3.9 %gather_fusion.2 = bf16[1024,256]{1,0:T(8,128)(2,1)S(1)} fusion(bf16[256,256]{1,0:T(8,128)(2,1)S(1)} %all_gather.7, s32[1024]{0:T(1024)S(1)} %fusion.36), kind=kCustom, calls=%fused_computation.1.clone | custom fusion | bytes 1052672 | tf_op jit(solution)/shard_map/jit(_take)/gather | solution.py:119
  53.2 0.2 copy.25
  53.4 1.9 %multiply_reduce_fusion = (f32[256]{0:T(256)}, f32[1024]{0:T(1024)S(1)}, f32[1024]{0:T(1024)S(1)}) fusion(bf16[1024,256]{0,1:T(8,128)(2,1)S(1)} %copy.24, f32[1024,256]{0,1:T(8,128)S(1)} %get-tuple-element.49, f32[1024]{0:T(1024)S(1)} %add_rsqrt_fusion, f32[1024]{0:T(1024)S(1)} %broadcast_multiply_fusion.2, f32[1024]{0:T(1024)S(1)} %fusion.35, ...), kind=kLoop, calls=%fused_computation.15 | loop fusion | flops 3405568 | bytes 2120704 | tf_op jit(solution)/shard_map/reduce_sum | solution.py:121
  55.3 1.5 multiply_convert_fusion
  56.8 1.1 fusion.52
  57.8 0.5 fusion.1
  58.4 0.5 copy-done.13
  58.9 0.2 copy-done.15
  59.0 0.2 copy-done.18
  59.2 1.5 fusion.10
  60.7 1.8 %fusion.49 = (bf16[1024,768]{1,0:T(8,128)(2,1)}, f32[1024,768]{1,0:T(8,128)S(1)}) fusion(bf16[1024,256]{1,0:T(8,128)(2,1)S(1)} %fusion.1, bf16[768,256]{1,0:T(8,128)(2,1)S(1)} %copy-done), kind=kOutput, calls=%fused_computation.99 | convolution fusion | flops 403439616 | bytes 5636096 | tf_op jit(solution)/shard_map/dot_general | solution.py:52
  62.5 0.1 slice.68
  62.5 0.3 copy.29
  62.9 0.1 fusion.4
  63.1 0.5 copy-done.27
  63.6 2.0 %convolution_convert_fusion = bf16[256,256]{1,0:T(8,128)(2,1)} fusion(bf16[1024,768]{1,0:T(8,128)(2,1)} %get-tuple-element.52, s32[1024]{0:T(1024)S(1)} %copy-done.27), kind=kOutput, calls=%fused_computation.10 | convolution fusion | flops 134545408 | bytes 659456 | tf_op jit(solution)/shard_map/dot_general | solution.py:137
  65.6 2.4 %fusion.50 = (bf16[512,256]{1,0:T(8,128)(2,1)S(1)}, f32[512,256]{1,0:T(8,128)}) fusion(bf16[1024,768]{1,0:T(8,128)(2,1)} %get-tuple-element.52, s32[1024]{0:T(1024)S(1)} %copy-done.31), kind=kOutput, calls=%fused_computation.100 | convolution fusion | flops 269090816 | bytes 1314816 | tf_op jit(solution)/shard_map/dot_general | solution.py:136
  68.0 3.6 %collective-permute-start.2 = (bf16[128,256]{1,0:T(8,128)(2,1)S(1)}, bf16[128,256]{1,0:T(8,128)(2,1)S(1)}, u32[]{:S(2)}, u32[]{:S(2)}) collective-permute-start(bf16[128,256]{1,0:T(8,128)(2,1)S(1)} %get-tuple-element.39), channel_id=1, source_target_pairs={{0,2},{2,4},{4,6},{6,8},{8,10},{10,12},{12,14},{14,16},{16,18},{18... | collective-permute-start | bytes 196616 | tf_op jit(solution)/shard_map/ppermute | solution.py:23
  71.6 1.3 collective-permute-start.3
  72.9 0.2 fusion.33
  73.2 1.0 copy.27
  74.2 1.0 copy.28
  75.2 0.0 reduce-scatter.8.cloned.1.call-update
  75.2 0.0 reduce-scatter.6.cloned.1.call-start
  75.3 2.4 %collective-permute-done.3 = bf16[128,256]{1,0:T(8,128)(2,1)S(1)} collective-permute-done((bf16[128,256]{1,0:T(8,128)(2,1)S(1)}, bf16[128,256]{1,0:T(8,128)(2,1)S(1)}, u32[]{:S(2)}, u32[]{:S(2)}) %collective-permute-start.3) | collective-permute-done | bytes 65568 | tf_op jit(solution)/shard_map/ppermute | solution.py:23
  77.7 1.0 fusion.32
  78.7 0.7 pad_maximum_fusion.5
  79.4 0.0 reduce-scatter.6.cloned.1.call-update
  79.5 64.1 %all-reduce.2 = (bf16[768,256]{1,0:T(8,128)(2,1)}, bf16[256,256]{1,0:T(8,128)(2,1)}, f32[256]{0:T(256)}, bf16[512,256]{1,0:T(8,128)(2,1)}, bf16[256,256]{1,0:T(8,128)(2,1)}, /*index=5*/f32[256]{0:T(256)}) all-reduce(f32[768,256]{1,0:T(8,128)S(1)} %copy-done.9, ...), channel_id=1, replica_groups=mesh['row'=16,'rep'=2] {'row','rep'}, use_global_device_ids=true, to_apply=%region_11.13 | all-reduce | flops 459264 | bytes 2756608 | tf_op jit(solution)/shard_map/psum | solution.py:154
  143.6 1.5 %fusion.29 = bf16[128,256]{1,0:T(8,128)(2,1)} fusion(bf16[128,256]{1,0:T(8,128)(2,1)S(1)} %copy-done.21, f32[128,512]{1,0:T(8,128)S(1)} %copy-done.8, bf16[128,256]{1,0:T(8,128)(2,1)} %reduce-scatter.8.cloned.1.call-done, bf16[128,256]{1,0:T(8,128)(2,1)} %reduce-scatter.6.cloned.1.call-done), kind=kLoop, calls=%fused_computation.55 | loop fusion | flops 229376 | bytes 393216 | tf_op jit(solution)/shard_map/convert_element_type | solution.py:153
  (85 shorter events, 0.3 us)
Async XLA Ops:
  7.2 20.3 %copy-start = (bf16[768,256]{1,0:T(8,128)(2,1)S(1)}, bf16[768,256]{1,0:T(8,128)(2,1)}, u32[]{:S(2)}) copy-start(bf16[768,256]{1,0:T(8,128)(2,1)} %param.20) | copy-start | bytes 1179652
  7.2 34.1 %reduce-scatter.4.cloned.1.call-start = ((), (), s32[]{:S(2)}) async-start(), calls=%async_computation.3 | async-start | bytes 393216 | tf_op jit(solution)/shard_map/reduce_scatter | solution.py:98
  9.6 13.6 %collective-permute-start = (bf16[128,256]{1,0:T(8,128)(2,1)S(1)}, bf16[128,256]{1,0:T(8,128)(2,1)S(1)}, u32[]{:S(2)}, u32[]{:S(2)}) collective-permute-start(bf16[128,256]{1,0:T(8,128)(2,1)S(1)} %get-tuple-element.42), channel_id=1, source_target_pairs={{0,2},{2,4},{4,6},{6,8},{8,10},{10,12},{12,14},{14,16},{16,18},{18... | collective-permute-start | bytes 196616 | tf_op jit(solution)/shard_map/ppermute | solution.py:14
  14.4 8.9 %collective-permute-start.1 = (bf16[128,256]{1,0:T(8,128)(2,1)S(1)}, bf16[128,256]{1,0:T(8,128)(2,1)S(1)}, u32[]{:S(2)}, u32[]{:S(2)}) collective-permute-start(bf16[128,256]{1,0:T(8,128)(2,1)S(1)} %get-tuple-element.43), channel_id=1, source_target_pairs={{2,0},{4,2},{6,4},{8,6},{10,8},{12,10},{14,12},{16,14},{18,16},{20... | collective-permute-start | bytes 196616 | tf_op jit(solution)/shard_map/ppermute | solution.py:15
  19.0 4.0 %copy-start.28 = (pred[1024]{0:T(1024)(128)(4,1)}, pred[1024]{0:T(1024)(128)(4,1)S(1)}, u32[]{:S(2)}) copy-start(pred[1024]{0:T(1024)(128)(4,1)S(1)} %get-tuple-element.33) | copy-start | bytes 3076
  19.0 10.6 %copy-start.26 = (s32[1024]{0:T(1024)}, s32[1024]{0:T(1024)S(1)}, u32[]{:S(2)}) copy-start(s32[1024]{0:T(1024)S(1)} %get-tuple-element.34) | copy-start | bytes 12292
  23.2 4.2 %copy-start.12 = (bf16[1024,256]{1,0:T(8,128)(2,1)}, bf16[1024,256]{1,0:T(8,128)(2,1)S(1)}, u32[]{:S(2)}) copy-start(bf16[1024,256]{1,0:T(8,128)(2,1)S(1)} %broadcast_select_fusion) | copy-start | bytes 1572868
  23.3 4.2 %copy-start.17 = (bf16[1024,256]{1,0:T(8,128)(2,1)S(1)}, bf16[1024,256]{1,0:T(8,128)(2,1)}, u32[]{:S(2)}) copy-start(bf16[1024,256]{1,0:T(8,128)(2,1)} %param.16) | copy-start | bytes 1572868
  27.5 1.6 %copy-start.14 = (bf16[1024,256]{1,0:T(8,128)(2,1)}, bf16[1024,256]{1,0:T(8,128)(2,1)S(1)}, u32[]{:S(2)}) copy-start(bf16[1024,256]{1,0:T(8,128)(2,1)S(1)} %broadcast_select_fusion.1) | copy-start | bytes 1572868
  27.5 1.6 %copy-start.24 = (bf16[256,256]{1,0:T(8,128)(2,1)S(1)}, bf16[256,256]{1,0:T(8,128)(2,1)}, u32[]{:S(2)}) copy-start(bf16[256,256]{1,0:T(8,128)(2,1)} %param.21) | copy-start | bytes 393220
  29.1 0.7 copy-start.33
  29.6 2.5 %copy-start.16 = (bf16[1024,256]{1,0:T(8,128)(2,1)S(1)}, bf16[1024,256]{1,0:T(8,128)(2,1)}, u32[]{:S(2)}) copy-start(bf16[1024,256]{1,0:T(8,128)(2,1)} %param.27) | copy-start | bytes 1572868
  30.9 11.2 %copy-start.3 = (bf16[512,256]{1,0:T(8,128)(2,1)S(1)}, bf16[512,256]{1,0:T(8,128)(2,1)}, u32[]{:S(2)}) copy-start(bf16[512,256]{1,0:T(8,128)(2,1)} %param.23) | copy-start | bytes 786436
  30.9 11.3 %copy-start.5 = (bf16[128,256]{1,0:T(8,128)(2,1)S(1)}, bf16[128,256]{1,0:T(8,128)(2,1)}, u32[]{:S(2)}) copy-start(bf16[128,256]{1,0:T(8,128)(2,1)} %param.15) | copy-start | bytes 196612
  31.0 12.8 %copy-start.20 = (bf16[128,256]{1,0:T(8,128)(2,1)S(1)}, bf16[128,256]{1,0:T(8,128)(2,1)}, u32[]{:S(2)}) copy-start(bf16[128,256]{1,0:T(8,128)(2,1)} %param.26) | copy-start | bytes 196612
  31.0 12.8 %copy-start.35 = (f32[256]{0:T(256)S(1)}, f32[256]{0:T(256)}, u32[]{:S(2)}) copy-start(f32[256]{0:T(256)} %param.25) | copy-start | bytes 3076
  31.0 112.6 %reduce-scatter.8.cloned.1.call-start = ((), (), s32[]{:S(2)}) async-start(), calls=%async_computation.5 | async-start | bytes 196608 | tf_op jit(solution)/shard_map/reduce_scatter | solution.py:148
  32.2 12.9 %copy-start.36 = (bf16[256,256]{1,0:T(8,128)(2,1)S(1)}, bf16[256,256]{1,0:T(8,128)(2,1)}, u32[]{:S(2)}) copy-start(bf16[256,256]{1,0:T(8,128)(2,1)} %param.24) | copy-start | bytes 393220
  42.2 3.2 %copy-start.10 = (bf16[128,256]{1,0:T(8,128)(2,1)}, bf16[128,256]{1,0:T(8,128)(2,1)S(1)}, u32[]{:S(2)}) copy-start(bf16[128,256]{1,0:T(8,128)(2,1)S(1)} %convert_element_type.98) | copy-start | bytes 196612
  45.4 3.8 %copy-start.22 = (bf16[128,256]{1,0:T(8,128)(2,1)}, bf16[128,256]{1,0:T(8,128)(2,1)S(1)}, u32[]{:S(2)}) copy-start(bf16[128,256]{1,0:T(8,128)(2,1)S(1)} %fusion.2) | copy-start | bytes 196612
  46.6 0.7 copy-start.7
  53.2 2.1 %copy-start.29 = (pred[1024]{0:T(1024)(128)(4,1)S(1)}, pred[1024]{0:T(1024)(128)(4,1)}, u32[]{:S(2)}) copy-start(pred[1024]{0:T(1024)(128)(4,1)} %copy-done.28) | copy-start | bytes 3076
  53.4 1.9 %copy-start.1 = (bf16[1024,256]{0,1:T(8,128)(2,1)S(1)}, bf16[1024,256]{0,1:T(8,128)(2,1)}, u32[]{:S(2)}) copy-start(bf16[1024,256]{0,1:T(8,128)(2,1)} %copy.23) | copy-start | bytes 1572868
  53.4 1.9 %copy-start.34 = (f32[256]{0:T(256)S(1)}, f32[256]{0:T(256)}, u32[]{:S(2)}) copy-start(f32[256]{0:T(256)} %param.22) | copy-start | bytes 3076
  55.3 2.5 %copy-start.25 = (bf16[256,256]{1,0:T(8,128)(2,1)S(1)}, bf16[256,256]{1,0:T(8,128)(2,1)}, u32[]{:S(2)}) copy-start(bf16[256,256]{1,0:T(8,128)(2,1)} %param.21) | copy-start | bytes 393220
  55.3 2.5 %copy-start.37 = (f32[1024,256]{1,0:T(8,128)S(1)}, f32[1024,256]{1,0:T(8,128)}, u32[]{:S(2)}) copy-start(f32[1024,256]{1,0:T(8,128)} %get-tuple-element.47) | copy-start | bytes 3145732
  57.8 1.0 copy-start.13
  57.8 1.2 copy-start.15
  57.8 1.4 copy-start.18
  62.9 0.7 copy-start.27
  62.9 2.7 %copy-start.31 = (s32[1024]{0:T(1024)S(1)}, s32[1024]{0:T(1024)}, u32[]{:S(2)}) copy-start(s32[1024]{0:T(1024)} %get-tuple-element.44) | copy-start | bytes 12292
  63.6 9.3 %copy-start.6 = (bf16[128,256]{1,0:T(8,128)(2,1)S(1)}, bf16[128,256]{1,0:T(8,128)(2,1)}, u32[]{:S(2)}) copy-start(bf16[128,256]{1,0:T(8,128)(2,1)} %param.15) | copy-start | bytes 196612
  63.6 9.3 %copy-start.11 = (bf16[128,256]{1,0:T(8,128)(2,1)S(1)}, bf16[128,256]{1,0:T(8,128)(2,1)}, u32[]{:S(2)}) copy-start(bf16[128,256]{1,0:T(8,128)(2,1)} %copy-done.10) | copy-start | bytes 196612
  63.6 9.3 %copy-start.23 = (bf16[128,256]{1,0:T(8,128)(2,1)S(1)}, bf16[128,256]{1,0:T(8,128)(2,1)}, u32[]{:S(2)}) copy-start(bf16[128,256]{1,0:T(8,128)(2,1)} %copy-done.22) | copy-start | bytes 196612
  65.6 7.5 %copy-start.2 = (bf16[1024,256]{0,1:T(8,128)(2,1)S(1)}, bf16[1024,256]{0,1:T(8,128)(2,1)}, u32[]{:S(2)}) copy-start(bf16[1024,256]{0,1:T(8,128)(2,1)} %get-tuple-element.36) | copy-start | bytes 1572868
  68.0 7.3 %collective-permute-start.2 = (bf16[128,256]{1,0:T(8,128)(2,1)S(1)}, bf16[128,256]{1,0:T(8,128)(2,1)S(1)}, u32[]{:S(2)}, u32[]{:S(2)}) collective-permute-start(bf16[128,256]{1,0:T(8,128)(2,1)S(1)} %get-tuple-element.39), channel_id=1, source_target_pairs={{0,2},{2,4},{4,6},{6,8},{8,10},{10,12},{12,14},{14,16},{16,18},{18... | collective-permute-start | bytes 196616 | tf_op jit(solution)/shard_map/ppermute | solution.py:23
  71.6 6.2 %collective-permute-start.3 = (bf16[128,256]{1,0:T(8,128)(2,1)S(1)}, bf16[128,256]{1,0:T(8,128)(2,1)S(1)}, u32[]{:S(2)}, u32[]{:S(2)}) collective-permute-start(bf16[128,256]{1,0:T(8,128)(2,1)S(1)} %get-tuple-element.40), channel_id=1, source_target_pairs={{2,0},{4,2},{6,4},{8,6},{10,8},{12,10},{14,12},{16,14},{18,16},{20... | collective-permute-start | bytes 196616 | tf_op jit(solution)/shard_map/ppermute | solution.py:23
  73.2 6.2 %copy-start.4 = (f32[256,256]{1,0:T(8,128)S(1)}, f32[256,256]{1,0:T(8,128)}, u32[]{:S(2)}) copy-start(f32[256,256]{1,0:T(8,128)} %fusion.52) | copy-start | bytes 786436
  73.2 6.2 %copy-start.9 = (f32[768,256]{1,0:T(8,128)S(1)}, f32[768,256]{1,0:T(8,128)}, u32[]{:S(2)}) copy-start(f32[768,256]{1,0:T(8,128)} %fusion.10) | copy-start | bytes 2359300
  73.2 6.2 %copy-start.19 = (f32[256,256]{1,0:T(8,128)S(1)}, f32[256,256]{1,0:T(8,128)}, u32[]{:S(2)}) copy-start(f32[256,256]{1,0:T(8,128)} %fusion.41) | copy-start | bytes 786436
  73.2 6.2 %copy-start.30 = (f32[256]{0:T(256)S(1)}, f32[256]{0:T(256)}, u32[]{:S(2)}) copy-start(f32[256]{0:T(256)} %get-tuple-element.21) | copy-start | bytes 3076
  73.2 6.2 %copy-start.32 = (f32[256]{0:T(256)S(1)}, f32[256]{0:T(256)}, u32[]{:S(2)}) copy-start(f32[256]{0:T(256)} %get-tuple-element.24) | copy-start | bytes 3076
  75.2 68.4 %copy-start.8 = (f32[128,512]{1,0:T(8,128)S(1)}, f32[128,512]{1,0:T(8,128)}, u32[]{:S(2)}) copy-start(f32[128,512]{1,0:T(8,128)} %copy-done.7) | copy-start | bytes 786436
  75.2 68.4 %copy-start.21 = (bf16[128,256]{1,0:T(8,128)(2,1)S(1)}, bf16[128,256]{1,0:T(8,128)(2,1)}, u32[]{:S(2)}) copy-start(bf16[128,256]{1,0:T(8,128)(2,1)} %param.26) | copy-start | bytes 196612
  75.2 68.4 %reduce-scatter.6.cloned.1.call-start = ((), (), s32[]{:S(2)}) async-start(), calls=%async_computation.4 | async-start | bytes 196608 | tf_op jit(solution)/shard_map/reduce_scatter | solution.py:146
Sparse Core Ops, SparseCore 0:
  31.1 10.1 reduce-scatter.3
  75.4 9.6 reduce-scatter.7
  87.3 8.7 reduce-scatter.5
where the time goes:
time: 152 us
  blocking collectives  68.4 us (45%)
  local copies, waits for them, and re-layouts  18 us (12%)
  matrix products  15.5 us (10%)
  between operations  15 us (10%)
  other arithmetic  12.3 us (8%)
  waiting for transfers between devices  11.5 us (8%)
  starting transfers between devices  11 us (7%)
    psum x1, blocking collectives, local(): lax.psum((d_w_edge_in, d_w_edge_out, d_gain_edge, d_w_node_in, d_w_node_o...  64.1 us
    reduce_scatter x1, waiting for transfers between devices, local(): lax.psum_scatter(partial_sums, 'rep', scatter_dimension=0, tiled=True)  9 us
    unnamed x81, local copies, waits for them, and re-layouts  5.84 us
    ppermute x2, starting transfers between devices, from_behind(): lax.ppermute(value, axis, [(source, source + steps) for source in range(f...  4.84 us
    ppermute x1, starting transfers between devices, padded(): before = lax.ppermute(last, axis, up)  4.74 us
    gather x2, local copies, waits for them, and re-layouts, local(): jnp.take(group_grad, recv_local, axis=0).astype(jnp.float32)  4.14 us
    gather x1, local copies, waits for them, and re-layouts, local(): jnp.take(grouped, recv_local, axis=0)  3.94 us
    gather x1, local copies, waits for them, and re-layouts, local(): jnp.take(extended, send_local, axis=0)  3.94 us
  transfers between devices with their start and end apart: 7, of which 2 were waited for; matrix products, arithmetic and copies ran while one was open for 8% of the time, Pallas kernels for 0%

commit v1 on v0

--- a/solution.py
+++ b/solution.py
@@ -1,7 +1,593 @@
+import functools
+
 import jax
 import jax.numpy as jnp
 from jax import lax
+from jax.experimental import pallas as pl
+from jax.experimental.pallas import tpu as pltpu
 from jax.sharding import PartitionSpec as P
+
+F32 = jnp.float32
+BF16 = jnp.bfloat16
+LANES = 128
+MESH = pl.DeviceIdType.MESH
+
+
+def mm(left, right):
+    return jnp.dot(left, right, preferred_element_type=F32)
+
+
+def contract_rows(left, right):
+    return lax.dot_general(left, right, (((0,), (0,)), ((), ())), preferred_element_type=F32)
+
+
+def times_transpose(left, right):
+    return lax.dot_general(left, right, (((1,), (1,)), ((), ())), preferred_element_type=F32)
+
+
+def sigmoid(v):
+    return 1.0 / (1.0 + jnp.exp(-v))
+
+
+def layer_norm(values):
+    centred = values - jnp.mean(values, axis=-1, keepdims=True)
+    inv_scale = lax.rsqrt(jnp.mean(centred * centred, axis=-1, keepdims=True) + 1e-05)
+    return (centred * inv_scale, inv_scale)
+
+
+def norm_back(upstream, normed, inv_scale):
+    return inv_scale * (
+        upstream
+        - jnp.mean(upstream, axis=-1, keepdims=True)
+        - normed * jnp.mean(upstream * normed, axis=-1, keepdims=True)
+    )
+
+
+def digits_of(n_row):
+    out, stride = [], 1
+    while stride < n_row:
+        radix = 4 if n_row % (stride * 4) == 0 else 2
+        out.append((stride, radix))
+        stride *= radix
+    return out
+
+
+def tree(values):
+    while len(values) > 1:
+        values = [values[i] + values[i + 1] for i in range(0, len(values), 2)]
+    return values[0]
+
+
+class Reduction:
+    def __init__(self, rank, digits, buf, recv_rep, recvs, gathered, sends, sems):
+        self.row, self.rep, self.digits = rank[0], rank[1], digits
+        self.buf, self.recv_rep, self.recvs, self.gathered = buf, recv_rep, recvs, gathered
+        self.send, self.recv = sends, sems
+        self.mine = [(self.row // s) % r for s, r in digits]
+        self.live = []
+        self.slot = 0
+
+    def partner(self, level, k):
+        stride, _ = self.digits[level]
+        d = self.mine[level]
+        other = jnp.bitwise_xor(d, k)
+        return self.row + (other - d) * stride, other
+
+    def copy(self, src, dst, device):
+        c = pltpu.make_async_remote_copy(
+            src_ref=src,
+            dst_ref=dst,
+            send_sem=self.send.at[self.slot],
+            recv_sem=self.recv.at[self.slot],
+            device_id=device,
+            device_id_type=MESH,
+        )
+        self.slot += 1
+        c.start()
+        self.live.append(c)
+
+    def wait(self):
+        for c in self.live:
+            c.wait()
+        self.live = []
+
+    def start_rep(self):
+        self.copy(self.buf.at[1 - self.rep], self.recv_rep, (self.row, 1 - self.rep))
+
+    def at(self, ref, level):
+        for d in self.mine[:level]:
+            ref = ref.at[d]
+        return ref
+
+    def add_rep(self):
+        self.wait()
+        self.buf[self.rep] = (self.buf[self.rep].astype(F32) + self.recv_rep[...].astype(F32)).astype(BF16)
+
+    def start_level(self, level):
+        ref = self.at(self.buf.at[self.rep], level)
+        for k in range(1, self.digits[level][1]):
+            row, other = self.partner(level, k)
+            self.copy(ref.at[other], self.recvs[level].at[k - 1], (row, self.rep))
+
+    def add_level(self, level):
+        self.wait()
+        ref = self.at(self.buf.at[self.rep], level + 1)
+        parts = [ref[...].astype(F32)]
+        parts += [self.recvs[level][k].astype(F32) for k in range(self.digits[level][1] - 1)]
+        total = tree(parts).astype(BF16)
+        if level + 1 == len(self.digits):
+            self.at(self.gathered.at[self.rep], level + 1)[...] = total
+        else:
+            ref[...] = total
+
+    def start_gather(self, level):
+        ref = self.at(self.gathered.at[self.rep], level + 1)
+        for k in range(1, self.digits[level][1]):
+            row, _ = self.partner(level, k)
+            self.copy(ref, ref, (row, self.rep))
+
+    def start_gather_rep(self):
+        self.copy(self.gathered.at[self.rep], self.gathered.at[self.rep], (self.row, 1 - self.rep))
+
+    def put(self, array, first):
+        block = self.buf.shape[-2]
+        _ = first
+        for h in range(2):
+            part = array[:, h * LANES : (h + 1) * LANES].astype(BF16)
+            self.buf[h] = part.reshape(self.buf.shape[1:])
+
+    def take(self, h):
+        full = self.gathered[h]
+        return full.reshape((-1, LANES))
+
+
+def kernel(
+    digits,
+    n_row,
+    chunk,
+    nf_ref, ef_ref, send_ref, recv_ref, count_ref,
+    wei_ref, weo_ref, ge_ref, wni_ref, wno_ref, gn_ref, dn_ref, de_ref,
+    nodes_out, edges_out, d_nodes, d_edges, o_wei, o_weo, o_ge, o_wni, o_wno, o_gn,
+    ext, table, cols, pre_s, norm_s, scale_s, act_s, psum, psum_in, grp_grad,
+    s_sum, r_sum, dwe, dwo, big_e, big_n, halo_out, halo_in, sib_out, sib_in,
+    gains, gains_in,
+    buf_n, rep_n, gat_n, buf_e, rep_e, gat_e,
+    send_sem, recv_sem, nsend, nrecv, esend, erecv, gsend, grecv,
+    *level_refs,
+):
+    row, rep = lax.axis_index("row"), lax.axis_index("rep")
+    sib = 1 - rep
+    shard, width = nf_ref.shape
+    edges = ef_ref.shape[0]
+    n_chunks = edges // chunk
+    levels = len(digits)
+    has_prev, has_next = row > 0, row < n_row - 1
+    red_n = Reduction((row, rep), digits, buf_n, rep_n, level_refs[:levels], gat_n, nsend, nrecv)
+    red_e = Reduction((row, rep), digits, buf_e, rep_e, level_refs[levels:], gat_e, esend, erecv)
+
+    def remote(src, dst, slot, device, there=None):
+        return pltpu.make_async_remote_copy(
+            src_ref=src, dst_ref=dst, send_sem=send_sem.at[slot],
+            recv_sem=recv_sem.at[slot if there is None else there],
+            device_id=device, device_id_type=MESH,
+        )
+
+    barrier = pltpu.get_barrier_semaphore()
+
+    def greet(device):
+        pl.semaphore_signal(barrier, inc=1, device_id=device, device_id_type=MESH)
+
+    greet((row, sib))
+    level_partners = 0
+    for level, (_, radix) in enumerate(digits):
+        for k in range(1, radix):
+            greet((red_n.partner(level, k)[0], rep))
+            level_partners += 1
+
+    @pl.when(has_prev)
+    def _():
+        for r in range(2):
+            greet((row - 1, r))
+
+    @pl.when(has_next)
+    def _():
+        for r in range(2):
+            greet((row + 1, r))
+
+    around = 2 * (jnp.int32(has_prev) + jnp.int32(has_next))
+    pl.semaphore_wait(barrier, 1 + level_partners + around)
+
+    own = 1 + rep
+    to_sib = remote(nf_ref, ext.at[own], 0, (row, sib))
+    to_sib.start()
+    goes = ((rep == 0) & has_prev) | ((rep == 1) & has_next)
+    target = jnp.where(rep == 0, row - 1, row + 1)
+    place = jnp.where(rep == 0, 3, 0)
+
+    def halo_copy(r):
+        return remote(nf_ref, ext.at[place], 1 + r, (target, r), there=jnp.where(rep == 0, 4, 3))
+
+    @pl.when(goes)
+    def _():
+        for r in range(2):
+            halo_copy(r).start()
+
+    ext[own] = nf_ref[...]
+
+    @pl.when(jnp.logical_not(has_prev))
+    def _():
+        ext[0] = jnp.zeros((shard, width), BF16)
+
+    @pl.when(jnp.logical_not(has_next))
+    def _():
+        ext[3] = jnp.zeros((shard, width), BF16)
+
+    group_start = row * (2 * shard)
+    send_row = send_ref[...] - (group_start - shard)
+    recv_row = recv_ref[...] - group_start
+    eight = lax.broadcasted_iota(jnp.int32, (8, edges), 0)
+    both = jnp.where(eight == 0, jnp.broadcast_to(send_row, (8, edges)), jnp.broadcast_to(recv_row, (8, edges)))
+    cols[...] = jnp.transpose(both)
+    count = count_ref[0]
+
+    def rows_of(c):
+        return pl.ds(pl.multiple_of(c * chunk, chunk), chunk)
+
+    def live_of(c):
+        slots = lax.broadcasted_iota(jnp.int32, (chunk, 1), 0) + c * chunk
+        return (slots < count).astype(F32)
+
+    def row_table(index, n):
+        return (lax.broadcasted_iota(jnp.int32, (n, chunk), 0) == index).astype(BF16)
+
+    def col_table(index, n):
+        return (lax.broadcasted_iota(jnp.int32, (chunk, n), 1) == index).astype(BF16)
+
+    def edge_part(c, carry):
+        at = rows_of(c)
+        pre_s[at, :] = mm(ef_ref[at, :], wei_ref[:width, :])
+        return carry
+
+    lax.fori_loop(0, n_chunks, edge_part, 0)
+    psum[...] = jnp.zeros_like(psum)
+
+    to_sib.wait()
+
+    @pl.when(goes)
+    def _():
+        for r in range(2):
+            halo_copy(r).wait_send()
+
+    @pl.when(has_prev)
+    def _():
+        remote(nf_ref, ext.at[0], 1, (row, sib), there=3).wait_recv()
+
+    @pl.when(has_next)
+    def _():
+        remote(nf_ref, ext.at[3], 1, (row, sib), there=4).wait_recv()
+
+    latents = ext[...].reshape((4 * shard, width))
+    group = latents[shard : 3 * shard]
+    table[: 4 * shard, :] = mm(latents, wei_ref[width : 2 * width, :]).astype(BF16)
+    table[4 * shard :, :] = mm(group, wei_ref[2 * width :, :]).astype(BF16)
+    gain_e = ge_ref[...]
+
+    def forward(c, carry):
+        at = rows_of(c)
+        s_col, r_col = cols[at, 0:1], cols[at, 1:2]
+        pre = (
+            pre_s[at, :]
+            + mm(col_table(s_col, 4 * shard), table[: 4 * shard, :])
+            + mm(col_table(r_col, 2 * shard), table[4 * shard :, :])
+        )
+        pre_s[at, :] = pre
+        act = (pre * sigmoid(pre)).astype(BF16)
+        act_s[at, :] = act
+        norm, scale = layer_norm(mm(act, weo_ref[...]))
+        norm_s[at, :] = norm
+        scale_s[at, :] = scale
+        message = live_of(c) * norm * gain_e
+        edges_out[at, :] = (ef_ref[at, :].astype(F32) + message).astype(BF16)
+        r_row = recv_ref[:, at] - group_start
+        sums = mm(row_table(r_row, 2 * shard), message.astype(BF16))
+        psum[...] += sums.reshape((2, shard, width))
+        return carry
+
+    lax.fori_loop(0, n_chunks, forward, 0)
+
+    agg_copy = remote(psum.at[sib], psum_in, 5, (row, sib))
+    agg_copy.start()
+    nf = nf_ref[...]
+    half_pre = mm(nf, wni_ref[:width, :])
+    s_sum[...] = jnp.zeros_like(s_sum)
+    r_sum[...] = jnp.zeros_like(r_sum)
+    dwe[...] = jnp.zeros_like(dwe)
+    dwo[...] = jnp.zeros_like(dwo)
+    agg_copy.wait()
+    agg = (psum[rep] + psum_in[...]).astype(BF16)
+    node_pre = half_pre + mm(agg, wni_ref[width:, :])
+    node_sig = sigmoid(node_pre)
+    node_act = (node_pre * node_sig).astype(BF16)
+    node_norm, node_scale = layer_norm(mm(node_act, wno_ref[...]))
+    gain_n = gn_ref[...]
+    grad = dn_ref[...].astype(F32)
+    d_mix = norm_back(grad * gain_n, node_norm, node_scale).astype(BF16)
+    slope = node_sig * (1.0 + node_pre * (1.0 - node_sig))
+    d_pre_n = (times_transpose(d_mix, wno_ref[...]) * slope).astype(BF16)
+    grp_grad[rep] = times_transpose(d_pre_n, wni_ref[width:, :]).astype(BF16)
+    grad_copy = remote(grp_grad.at[rep], grp_grad.at[rep], 6, (row, sib))
+    grad_copy.start()
+    big_n[:width, :] = contract_rows(nf, d_pre_n)
+    big_n[width : 2 * width, :] = contract_rows(agg, d_pre_n)
+    big_n[2 * width : 3 * width, :] = contract_rows(node_act, d_mix)
+    if big_n.shape[0] > 3 * width:
+        big_n[3 * width :, :] = jnp.zeros((big_n.shape[0] - 3 * width, width), F32)
+    red_n.put(big_n, 0)
+    red_n.start_rep()
+    nodes_out[...] = (nf.astype(F32) + node_norm * gain_n).astype(BF16)
+    gains[0, 1:2, :] = jnp.sum(grad * node_norm, axis=0, keepdims=True)
+    gains[0, 0:1, :] = jnp.zeros((1, width), F32)
+    direct = grad + times_transpose(d_pre_n, wni_ref[:width, :])
+    grad_copy.wait()
+
+    def backward(c, carry):
+        at = rows_of(c)
+        group_grad = grp_grad[...].reshape((2 * shard, width))
+        d_out = de_ref[at, :].astype(F32)
+        d_msg = live_of(c) * (d_out + mm(col_table(cols[at, 1:2], 2 * shard), group_grad))
+        norm = norm_s[at, :]
+        gains[0, 0:1, :] += jnp.sum(d_msg * norm, axis=0, keepdims=True)
+        d_mix_e = norm_back(d_msg * gain_e, norm, scale_s[at, :]).astype(BF16)
+        dwo[...] += contract_rows(act_s[at, :], d_mix_e)
+        pre = pre_s[at, :]
+        sig = sigmoid(pre)
+        d_pre = (
+            times_transpose(d_mix_e, weo_ref[...]) * (sig * (1.0 + pre * (1.0 - sig)))
+        ).astype(BF16)
+        dwe[...] += contract_rows(ef_ref[at, :], d_pre)
+        s_row = send_ref[:, at] - (group_start - shard)
+        r_row = recv_ref[:, at] - group_start
+        s_sum[...] += mm(row_table(s_row, 4 * shard), d_pre)
+        r_sum[...] += mm(row_table(r_row, 2 * shard), d_pre)
+        d_edges[at, :] = (d_out + times_transpose(d_pre, wei_ref[:width, :])).astype(BF16)
+        return carry
+
+    half = (n_chunks + 1) // 2
+    lax.fori_loop(0, half, backward, 0)
+    red_n.add_rep()
+    red_n.start_level(0)
+    lax.fori_loop(half, n_chunks, backward, 0)
+
+    sends_b = s_sum[...].astype(BF16)
+    recvs_b = r_sum[...].astype(BF16)
+    latents = ext[...].reshape((4 * shard, width))
+    big_e[:width, :] = dwe[...]
+    big_e[width : 2 * width, :] = contract_rows(latents, sends_b)
+    big_e[2 * width : 3 * width, :] = contract_rows(latents[shard : 3 * shard], recvs_b)
+    big_e[3 * width : 4 * width, :] = dwo[...]
+    if big_e.shape[0] > 4 * width:
+        big_e[4 * width :, :] = jnp.zeros((big_e.shape[0] - 4 * width, width), F32)
+    red_e.put(big_e, 0)
+    red_e.start_rep()
+
+    slot = [0]
+
+    def gain_start(devices):
+        out = []
+        stage = gain_start.stage
+        for device in devices:
+            c = pltpu.make_async_remote_copy(
+                src_ref=gains.at[stage], dst_ref=gains_in.at[slot[0]],
+                send_sem=gsend.at[slot[0]], recv_sem=grecv.at[slot[0]],
+                device_id=device, device_id_type=MESH,
+            )
+            c.start()
+            out.append((c, slot[0]))
+            slot[0] += 1
+        return out
+
+    gain_start.stage = 0
+
+    def gain_add(copies):
+        for c, _ in copies:
+            c.wait()
+        stage = gain_start.stage
+        gains[stage + 1] = tree([gains[stage]] + [gains_in[s] for _, s in copies])
+        gain_start.stage += 1
+
+    going = gain_start([(row, sib)])
+
+    sender = times_transpose(sends_b, wei_ref[width : 2 * width, :])
+    receiver = times_transpose(recvs_b, wei_ref[2 * width :, :])
+    halo_out[0] = sender[:shard].astype(BF16)
+    halo_out[1] = sender[3 * shard :].astype(BF16)
+
+    def to_prev():
+        return remote(halo_out.at[0], halo_in.at[rep], 7, (row - 1, 1), there=9 + rep)
+
+    def to_next():
+        return remote(halo_out.at[1], halo_in.at[rep], 8, (row + 1, 0), there=9 + rep)
+
+    @pl.when(has_prev)
+    def _():
+        to_prev().start()
+
+    @pl.when(has_next)
+    def _():
+        to_next().start()
+
+    inner = sender[shard : 3 * shard] + receiver
+    sib_out[...] = inner.reshape((2, shard, width))
+    sib_copy = remote(sib_out.at[sib], sib_in, 11, (row, sib))
+    sib_copy.start()
+
+    red_n.add_level(0)
+    for level in range(1, levels):
+        red_n.start_level(level)
+        if level == 1:
+            red_e.add_rep()
+            gain_add(going)
+            red_e.start_level(0)
+            going = gain_start([(red_e.partner(0, k)[0], rep) for k in range(1, digits[0][1])])
+        red_n.add_level(level)
+    red_n.start_gather(levels - 1)
+
+    sib_copy.wait()
+    total = direct + sib_out[rep] + sib_in[...]
+
+    @pl.when(has_prev)
+    def _():
+        to_prev().wait_send()
+
+    @pl.when(has_next)
+    def _():
+        to_next().wait_send()
+
+    hears = ((rep == 0) & has_prev) | ((rep == 1) & has_next)
+
+    @pl.when(hears)
+    def _():
+        for r in range(2):
+            remote(halo_out.at[0], halo_in.at[r], 7, (row, sib), there=9 + r).wait_recv()
+        d_nodes[...] = (total + (halo_in[0].astype(F32) + halo_in[1].astype(F32))).astype(BF16)
+
+    @pl.when(jnp.logical_not(hears))
+    def _():
+        d_nodes[...] = total.astype(BF16)
+
+    if levels == 1:
+        red_e.add_rep()
+        gain_add(going)
+        red_e.start_level(0)
+        going = gain_start([(red_e.partner(0, k)[0], rep) for k in range(1, digits[0][1])])
+    red_n.wait()
+    if levels > 1:
+        red_n.start_gather(levels - 2)
+    for level in range(levels):
+        red_e.add_level(level)
+        gain_add(going)
+        if level + 1 < levels:
+            red_e.start_level(level + 1)
+            going = gain_start(
+                [(red_e.partner(level + 1, k)[0], rep) for k in range(1, digits[level + 1][1])]
+            )
+    for level in reversed(range(levels)):
+        red_e.start_gather(level)
+        if level < levels - 1:
+            red_n.wait()
+            if level > 0:
+                red_n.start_gather(level - 1)
+            else:
+                red_n.start_gather_rep()
+        red_e.wait()
+    if levels == 1:
+        red_n.start_gather_rep()
+    red_e.start_gather_rep()
+    o_ge[...] = gains[levels + 1, 0:1, :]
+    o_gn[...] = gains[levels + 1, 1:2, :]
+    red_n.wait()
+    for h in range(2):
+        lanes = slice(h * LANES, (h + 1) * LANES)
+        full = red_n.take(h)
+        o_wni[:, lanes] = full[: 2 * width]
+        o_wno[:, lanes] = full[2 * width : 3 * width]
+    red_e.wait()
+    for h in range(2):
+        lanes = slice(h * LANES, (h + 1) * LANES)
+        full = red_e.take(h)
+        o_wei[:, lanes] = full[: 3 * width]
+        o_weo[:, lanes] = full[3 * width : 4 * width]
+
+
+def local(
+    n_row,
+    node_feats, edge_feats, senders, receivers, edge_count,
+    w_edge_in, w_edge_out, gain_edge, w_node_in, w_node_out, gain_node,
+    d_nodes_out, d_edges_out,
+):
+    shard, width = node_feats.shape
+    edges = edge_feats.shape[0]
+    chunk = min(edges, 256)
+    digits = digits_of(n_row)
+    radices = tuple(r for _, r in digits)
+    partners = sum(r - 1 for r in radices)
+    vmem, smem = pl.BlockSpec(memory_space=pltpu.VMEM), pl.BlockSpec(memory_space=pltpu.SMEM)
+
+    def reduction(rows):
+        block = -(-rows // (16 * n_row)) * 16
+        tail = (block, LANES)
+        levels = [
+            pltpu.VMEM((r - 1,) + radices[i + 1 :] + tail, BF16) for i, r in enumerate(radices)
+        ]
+        return (
+            block * n_row,
+            [pltpu.VMEM((2,) + radices + tail, BF16), pltpu.VMEM(radices + tail, BF16),
+             pltpu.VMEM((2,) + radices + tail, BF16)],
+            levels,
+        )
+
+    rows_n, bufs_n, levels_n = reduction(3 * width)
+    rows_e, bufs_e, levels_e = reduction(4 * width)
+    copies = 2 * (1 + partners)
+    dma = pltpu.SemaphoreType.DMA
+    scratch = [
+        pltpu.VMEM((4, shard, width), BF16),
+        pltpu.VMEM((6 * shard, width), BF16),
+        pltpu.VMEM((edges, 8), jnp.int32),
+        pltpu.VMEM((edges, width), F32),
+        pltpu.VMEM((edges, width), F32),
+        pltpu.VMEM((edges, 1), F32),
+        pltpu.VMEM((edges, width), BF16),
+        pltpu.VMEM((2, shard, width), F32),
+        pltpu.VMEM((shard, width), F32),
+        pltpu.VMEM((2, shard, width), BF16),
+        pltpu.VMEM((4 * shard, width), F32),
+        pltpu.VMEM((2 * shard, width), F32),
+        pltpu.VMEM((width, width), F32),
+        pltpu.VMEM((width, width), F32),
+        pltpu.VMEM((rows_e, width), F32),
+        pltpu.VMEM((rows_n, width), F32),
+        pltpu.VMEM((2, shard, width), BF16),
+        pltpu.VMEM((2, shard, width), BF16),
+        pltpu.VMEM((2, shard, width), F32),
+        pltpu.VMEM((shard, width), F32),
+        pltpu.VMEM((len(digits) + 2, 8, width), F32),
+        pltpu.VMEM((1 + partners, 8, width), F32),
+        *bufs_n,
+        *bufs_e,
+        dma((12,)), dma((12,)),
+        dma((copies,)), dma((copies,)), dma((copies,)), dma((copies,)),
+        dma((1 + partners,)), dma((1 + partners,)),
+        *levels_n,
+        *levels_e,
+    ]
+    out = pl.pallas_call(
+        functools.partial(kernel, digits, n_row, chunk),
+        out_shape=(
+            jax.ShapeDtypeStruct((shard, width), BF16),
+            jax.ShapeDtypeStruct((edges, width), BF16),
+            jax.ShapeDtypeStruct((shard, width), BF16),
+            jax.ShapeDtypeStruct((edges, width), BF16),
+            jax.ShapeDtypeStruct(w_edge_in.shape, BF16),
+            jax.ShapeDtypeStruct(w_edge_out.shape, BF16),
+            jax.ShapeDtypeStruct((1, width), F32),
+            jax.ShapeDtypeStruct(w_node_in.shape, BF16),
+            jax.ShapeDtypeStruct(w_node_out.shape, BF16),
+            jax.ShapeDtypeStruct((1, width), F32),
+        ),
+        in_specs=[vmem] * 4 + [smem] + [vmem] * 8,
+        out_specs=tuple([vmem] * 10),
+        scratch_shapes=scratch,
+        compiler_params=pltpu.CompilerParams(
+            collective_id=0, has_side_effects=True, vmem_limit_bytes=60 * 2**20
+        ),
+        name="layer",
+    )(
+        node_feats, edge_feats, senders[None, :], receivers[None, :], edge_count,
+        w_edge_in, w_edge_out, gain_edge[None, :], w_node_in, w_node_out, gain_node[None, :],
+        d_nodes_out, d_edges_out,
+    )
+    return (*out[:6], out[6][0], *out[7:9], out[9][0])
 
 
 def padded(x, sides, width):
@@ -23,18 +609,18 @@
     return lax.ppermute(value, axis, [(source, source + steps) for source in range(first, last)])
 
 
-def silu_slope(pre):
+def plain_slope(pre):
     sigmoid = jax.nn.sigmoid(pre)
     return sigmoid * (1.0 + pre * (1.0 - sigmoid))
 
 
-def layer_norm(values):
+def plain_norm(values):
     centred = values - jnp.mean(values, axis=-1, keepdims=True)
     inv_scale = lax.rsqrt(jnp.mean(centred * centred, axis=-1, keepdims=True) + 1e-05)
     return (centred * inv_scale, inv_scale)
 
 
-def norm_back(upstream, normed, inv_scale):
+def plain_back(upstream, normed, inv_scale):
     return inv_scale * (
         upstream
         - jnp.mean(upstream, axis=-1, keepdims=True)
@@ -42,19 +628,19 @@
     )
 
 
-def contract_rows(left, right):
+def plain_rows(left, right):
     return lax.dot_general(
         left, right, (((0,), (0,)), ((), ())), preferred_element_type=jnp.float32
     )
 
 
-def times_transpose(left, right):
+def plain_times(left, right):
     return lax.dot_general(
         left, right, (((1,), (1,)), ((), ())), preferred_element_type=jnp.float32
     )
 
 
-def local(
+def plain(
     node_feats,
     edge_feats,
     senders,
@@ -87,7 +673,7 @@
     edge_pre = jnp.dot(edge_input, w_edge_in, preferred_element_type=jnp.float32)
     edge_act = jax.nn.silu(edge_pre).astype(jnp.bfloat16)
     edge_mix = jnp.dot(edge_act, w_edge_out, preferred_element_type=jnp.float32)
-    edge_norm, edge_scale = layer_norm(edge_mix)
+    edge_norm, edge_scale = plain_norm(edge_mix)
     message = live_mask * edge_norm * gain_edge
     edges_out = (edge_feats.astype(jnp.float32) + message).astype(jnp.bfloat16)
     message_b = message.astype(jnp.bfloat16)
@@ -100,17 +686,17 @@
     node_pre = jnp.dot(node_input, w_node_in, preferred_element_type=jnp.float32)
     node_act = jax.nn.silu(node_pre).astype(jnp.bfloat16)
     node_mix = jnp.dot(node_act, w_node_out, preferred_element_type=jnp.float32)
-    node_norm, node_scale = layer_norm(node_mix)
+    node_norm, node_scale = plain_norm(node_mix)
     nodes_out = (node_feats.astype(jnp.float32) + node_norm * gain_node).astype(jnp.bfloat16)
     grad_nodes = d_nodes_out.astype(jnp.float32)
     d_gain_node = jnp.sum(grad_nodes * node_norm, axis=0)
-    d_node_mix = norm_back(grad_nodes * gain_node, node_norm, node_scale).astype(jnp.bfloat16)
-    d_w_node_out = contract_rows(node_act, d_node_mix)
-    d_node_pre = (times_transpose(d_node_mix, w_node_out) * silu_slope(node_pre)).astype(
+    d_node_mix = plain_back(grad_nodes * gain_node, node_norm, node_scale).astype(jnp.bfloat16)
+    d_w_node_out = plain_rows(node_act, d_node_mix)
+    d_node_pre = (plain_times(d_node_mix, w_node_out) * plain_slope(node_pre)).astype(
         jnp.bfloat16
     )
-    d_w_node_in = contract_rows(node_input, d_node_pre)
-    d_node_input = times_transpose(d_node_pre, w_node_in)
+    d_w_node_in = plain_rows(node_input, d_node_pre)
+    d_node_input = plain_times(d_node_pre, w_node_in)
     d_aggregate = d_node_input[:, width:].astype(jnp.bfloat16)
     d_direct = grad_nodes + d_node_input[:, :width]
     group_grad = lax.all_gather(d_aggregate, "rep", axis=0, tiled=True)
@@ -119,13 +705,13 @@
         + jnp.take(group_grad, recv_local, axis=0).astype(jnp.float32)
     )
     d_gain_edge = jnp.sum(d_message * edge_norm, axis=0)
-    d_edge_mix = norm_back(d_message * gain_edge, edge_norm, edge_scale).astype(jnp.bfloat16)
-    d_w_edge_out = contract_rows(edge_act, d_edge_mix)
-    d_edge_pre = (times_transpose(d_edge_mix, w_edge_out) * silu_slope(edge_pre)).astype(
+    d_edge_mix = plain_back(d_message * gain_edge, edge_norm, edge_scale).astype(jnp.bfloat16)
+    d_w_edge_out = plain_rows(edge_act, d_edge_mix)
+    d_edge_pre = (plain_times(d_edge_mix, w_edge_out) * plain_slope(edge_pre)).astype(
         jnp.bfloat16
     )
-    d_w_edge_in = contract_rows(edge_input, d_edge_pre)
-    d_edge_input = times_transpose(d_edge_pre, w_edge_in)
+    d_w_edge_in = plain_rows(edge_input, d_edge_pre)
+    d_edge_input = plain_times(d_edge_pre, w_edge_in)
     d_edges = (d_edges_out.astype(jnp.float32) + d_edge_input[:, :width]).astype(jnp.bfloat16)
     d_sender = d_edge_input[:, width : 2 * width].astype(jnp.bfloat16)
     d_receiver = d_edge_input[:, 2 * width :].astype(jnp.bfloat16)
@@ -170,35 +756,12 @@
 
 
 def solution(mesh):
+    split, flat, whole = P(("row", "rep"), None), P(("row", "rep")), P()
+    layer = functools.partial(local, mesh.shape["row"]) if mesh.shape["rep"] == 2 else plain
     return jax.shard_map(
-        local,
+        layer,
         mesh=mesh,
-        in_specs=(
-            P(("row", "rep"), None),
-            P(("row", "rep"), None),
-            P(("row", "rep")),
-            P(("row", "rep")),
-            P(("row", "rep")),
-            P(),
-            P(),
-            P(),
-            P(),
-            P(),
-            P(),
-            P(("row", "rep"), None),
-            P(("row", "rep"), None),
-        ),
-        out_specs=(
-            P(("row", "rep"), None),
-            P(("row", "rep"), None),
-            P(("row", "rep"), None),
-            P(("row", "rep"), None),
-            P(),
-            P(),
-            P(),
-            P(),
-            P(),
-            P(),
-        ),
+        in_specs=(split, split, flat, flat, flat) + (whole,) * 6 + (split, split),
+        out_specs=(split,) * 4 + (whole,) * 6,
         check_vma=False,
     )

time: 152 us -> 59.3 us (0.39)
  blocking collectives: 68.4 us -> 0 us
  Pallas kernels: 0 us -> 48 us
  matrix products: 15.5 us -> 0 us
  between operations: 15 us -> 1.31 us
  other arithmetic: 12.3 us -> 0 us
  waiting for transfers between devices: 11.5 us -> 0 us
  starting transfers between devices: 11 us -> 0 us
  local copies, waits for them, and re-layouts: 18 us -> 9.66 us
    psum x1 -> x0, blocking collectives: 64.1 us -> none  [local(): lax.psum((d_w_edge_in, d_w_edge_out, d_gain_edge, d_w_node_in, d_w_node_o...]
    pallas_call x0 -> x1, Pallas kernels: none -> 48 us  [local(): pl.pallas_call(functools.partial(kernel, digits, n_row, chunk), out_shape...]
    dot_general x15 -> x0, matrix products: 15.5 us -> none  [the longest x4 3.82 us: contract_rows(): lax.dot_general(left, right, (((0,), (0,)), ((), ())), preferred_element_...]
    gather x4 -> x0, local copies, waits for them, and re-layouts: 12 us -> none  [the longest x2 4.14 us: local(): jnp.take(group_grad, recv_local, axis=0).astype(jnp.float32)]
    ppermute x4 -> x0, starting transfers between devices: 10.9 us -> none  [the longest x2 4.84 us: from_behind(): lax.ppermute(value, axis, [(source, source + steps) for source in range(f...]
    reduce_scatter x3 -> x0, waiting for transfers between devices: 9 us -> none  [the longest x1 9 us: local(): lax.psum_scatter(partial_sums, 'rep', scatter_dimension=0, tiled=True)]
    all_gather x2 -> x0, blocking collectives: 4.27 us -> none  [the longest x1 2.38 us: local(): grouped = lax.all_gather(node_feats, 'rep', axis=0, tiled=True)]
    convert_element_type x5 -> x0, other arithmetic: 4.04 us -> none  [the longest x1 1.53 us: local(): d_nodes = (d_direct + edge_terms).astype(jnp.bfloat16)]
  transfers between devices with their start and end apart: 7 -> 0, of which waited for: 2 -> 0; matrix products, arithmetic and copies ran while one was open for 8% -> 0% of each run, Pallas kernels for 0% -> 0%
where the time goes in v1:
time: 59.3 us; the launch traced here: 59 us
  Pallas kernels  48 us (81%)
  local copies, waits for them, and re-layouts  9.66 us (16%)
  between operations  1.31 us (2%)
    pallas_call x1, Pallas kernels, local(): pl.pallas_call(functools.partial(kernel, digits, n_row, chunk), out_shape...  48 us
    unnamed x26, local copies, waits for them, and re-layouts  9.66 us

profile of v1, /device:TPU:0, one launch (start us, length us, event | category | flops | bytes accessed | tf_op | source)
XLA Modules:
  0.0 59.0 jit_solution(11669321036157266124)
XLA Ops:
  1.3 48.0 %layer.1 = (bf16[128,256]{1,0:T(8,128)(2,1)}, bf16[1024,256]{1,0:T(8,128)(2,1)}, bf16[128,256]{1,0:T(8,128)(2,1)}, bf16[1024,256]{1,0:T(8,128)(2,1)}, bf16[768,2...) custom-call(bf16[128,256]{1,0:T(8,128)(2,1)} %nf_ref.1, ...), custom_call_target="tpu_custom_call" | custom-call | tf_op jit(solution)/shard_map/layer/pallas_call | solution.py:564
  49.3 1.5 %copy.34 = bf16[128,256]{1,0:T(8,128)(2,1)} copy(bf16[128,256]{1,0:T(8,128)(2,1)} %get-tuple-element.40) | data formatting | bytes 131072
  50.8 0.0 copy-start.5
  50.8 0.0 copy-start
  50.8 1.9 %copy.35 = bf16[1024,256]{1,0:T(8,128)(2,1)} copy(bf16[1024,256]{1,0:T(8,128)(2,1)} %get-tuple-element.41) | data formatting | bytes 1048576
  52.7 0.0 copy-done.5
  52.7 0.6 %copy.36 = bf16[128,256]{1,0:T(8,128)(2,1)} copy(bf16[128,256]{1,0:T(8,128)(2,1)S(1)} %copy-done.5) | data formatting | bytes 131072
  53.3 0.0 copy-done
  53.3 0.0 copy-start.1
  53.3 0.8 %copy.37 = bf16[1024,256]{1,0:T(8,128)(2,1)} copy(bf16[1024,256]{1,0:T(8,128)(2,1)S(1)} %copy-done) | data formatting | bytes 1048576
  54.1 0.4 copy-done.1
  54.5 0.0 copy-start.4
  54.5 0.0 copy-start.7
  54.5 0.7 %copy.38 = bf16[768,256]{1,0:T(8,128)(2,1)} copy(bf16[768,256]{1,0:T(8,128)(2,1)S(1)} %copy-done.1) | data formatting | bytes 786432
  55.3 0.2 copy-done.4
  55.5 0.0 copy-start.2
  55.5 0.7 %copy.39 = bf16[256,256]{1,0:T(8,128)(2,1)} copy(bf16[256,256]{1,0:T(8,128)(2,1)S(1)} %copy-done.4) | data formatting | bytes 262144
  56.2 0.0 copy-done.7
  56.2 0.6 copy.40
  56.8 0.0 copy-done.2
  56.8 0.0 copy-start.3
  56.8 0.7 %copy.41 = bf16[512,256]{1,0:T(8,128)(2,1)} copy(bf16[512,256]{1,0:T(8,128)(2,1)S(1)} %copy-done.2) | data formatting | bytes 524288
  57.5 0.3 copy-done.3
  57.8 0.0 copy-start.6
  57.8 0.7 %copy.42 = bf16[256,256]{1,0:T(8,128)(2,1)} copy(bf16[256,256]{1,0:T(8,128)(2,1)S(1)} %copy-done.3) | data formatting | bytes 262144
  58.4 0.0 copy-done.6
  58.4 0.6 copy.43
Async XLA Ops:
  50.8 1.9 %copy-start.5 = (bf16[128,256]{1,0:T(8,128)(2,1)S(1)}, bf16[128,256]{1,0:T(8,128)(2,1)}, u32[]{:S(2)}) copy-start(bf16[128,256]{1,0:T(8,128)(2,1)} %get-tuple-element.42) | copy-start | bytes 196612
  50.8 2.6 %copy-start = (bf16[1024,256]{1,0:T(8,128)(2,1)S(1)}, bf16[1024,256]{1,0:T(8,128)(2,1)}, u32[]{:S(2)}) copy-start(bf16[1024,256]{1,0:T(8,128)(2,1)} %get-tuple-element.43) | copy-start | bytes 1572868
  53.3 1.2 %copy-start.1 = (bf16[768,256]{1,0:T(8,128)(2,1)S(1)}, bf16[768,256]{1,0:T(8,128)(2,1)}, u32[]{:S(2)}) copy-start(bf16[768,256]{1,0:T(8,128)(2,1)} %get-tuple-element.44) | copy-start | bytes 1179652
  54.5 1.0 %copy-start.4 = (bf16[256,256]{1,0:T(8,128)(2,1)S(1)}, bf16[256,256]{1,0:T(8,128)(2,1)}, u32[]{:S(2)}) copy-start(bf16[256,256]{1,0:T(8,128)(2,1)} %get-tuple-element.45) | copy-start | bytes 393220
  54.5 1.7 %copy-start.7 = (f32[1,256]{1,0:T(1,128)S(1)}, f32[1,256]{1,0:T(1,128)}, u32[]{:S(2)}) copy-start(f32[1,256]{1,0:T(1,128)} %get-tuple-element.26) | copy-start | bytes 3076
  55.5 1.2 %copy-start.2 = (bf16[512,256]{1,0:T(8,128)(2,1)S(1)}, bf16[512,256]{1,0:T(8,128)(2,1)}, u32[]{:S(2)}) copy-start(bf16[512,256]{1,0:T(8,128)(2,1)} %get-tuple-element.47) | copy-start | bytes 786436
  56.8 1.0 %copy-start.3 = (bf16[256,256]{1,0:T(8,128)(2,1)S(1)}, bf16[256,256]{1,0:T(8,128)(2,1)}, u32[]{:S(2)}) copy-start(bf16[256,256]{1,0:T(8,128)(2,1)} %get-tuple-element.48) | copy-start | bytes 393220
  57.8 0.7 %copy-start.6 = (f32[1,256]{1,0:T(1,128)S(1)}, f32[1,256]{1,0:T(1,128)}, u32[]{:S(2)}) copy-start(f32[1,256]{1,0:T(1,128)} %get-tuple-element.29) | copy-start | bytes 3076

commit v2 on v1

--- a/solution.py
+++ b/solution.py
@@ -92,7 +92,10 @@
         self.live = []
 
     def start_rep(self):
-        self.copy(self.buf.at[1 - self.rep], self.recv_rep, (self.row, 1 - self.rep))
+        d, radix = self.mine[0], self.digits[0][1]
+        for k in [*range(1, radix), 0]:
+            block = jnp.bitwise_xor(d, k)
+            self.copy(self.buf.at[1 - self.rep, block], self.recv_rep.at[block], (self.row, 1 - self.rep))
 
     def at(self, ref, level):
         for d in self.mine[:level]:
@@ -100,8 +103,15 @@
         return ref
 
     def add_rep(self):
-        self.wait()
-        self.buf[self.rep] = (self.buf[self.rep].astype(F32) + self.recv_rep[...].astype(F32)).astype(BF16)
+        arriving, self.live = self.live, []
+        d, radix = self.mine[0], self.digits[0][1]
+        for c, k in zip(arriving, [*range(1, radix), 0]):
+            c.wait()
+            block = jnp.bitwise_xor(d, k)
+            mine = self.buf.at[self.rep, block]
+            mine[...] = (mine[...].astype(F32) + self.recv_rep[block].astype(F32)).astype(BF16)
+            if k:
+                self.copy(mine, self.recvs[0].at[k - 1], (self.partner(0, k)[0], self.rep))
 
     def start_level(self, level):
         ref = self.at(self.buf.at[self.rep], level)
@@ -126,32 +136,38 @@
             row, _ = self.partner(level, k)
             self.copy(ref, ref, (row, self.rep))
 
-    def start_gather_rep(self):
-        self.copy(self.gathered.at[self.rep], self.gathered.at[self.rep], (self.row, 1 - self.rep))
-
-    def put(self, array, first):
-        block = self.buf.shape[-2]
-        _ = first
+    def start_gather_last(self):
+        self.start_gather(0)
+        ref = self.gathered.at[self.rep, self.mine[0]]
+        self.copy(ref, ref, (self.row, 1 - self.rep))
+
+    def forward(self):
+        radix = self.digits[0][1]
+        arriving, self.live = self.live[: radix - 1], self.live[radix - 1 :]
+        for c, k in zip(arriving, range(1, radix)):
+            c.wait()
+            ref = self.gathered.at[self.rep, jnp.bitwise_xor(self.mine[0], k)]
+            self.copy(ref, ref, (self.row, 1 - self.rep))
+
+    def put(self, array):
         for h in range(2):
             part = array[:, h * LANES : (h + 1) * LANES].astype(BF16)
             self.buf[h] = part.reshape(self.buf.shape[1:])
-
-    def take(self, h):
-        full = self.gathered[h]
-        return full.reshape((-1, LANES))
 
 
 def kernel(
     digits,
     n_row,
     chunk,
-    nf_ref, ef_ref, send_ref, recv_ref, count_ref,
-    wei_ref, weo_ref, ge_ref, wni_ref, wno_ref, gn_ref, dn_ref, de_ref,
-    nodes_out, edges_out, d_nodes, d_edges, o_wei, o_weo, o_ge, o_wni, o_wno, o_gn,
+    h_nf, h_ef, h_send, h_recv, count_ref,
+    h_wei, h_weo, h_ge, h_wni, h_wno, h_gn, h_dn, h_de,
+    nodes_out, edges_out, d_nodes, d_edges, gat_e, gat_n, o_gains,
+    nf_ref, ef_ref, send_ref, recv_ref,
+    wei_ref, weo_ref, ge_ref, wni_ref, wno_ref, gn_ref, dn_ref, de_ref, load_sem,
     ext, table, cols, pre_s, norm_s, scale_s, act_s, psum, psum_in, grp_grad,
     s_sum, r_sum, dwe, dwo, big_e, big_n, halo_out, halo_in, sib_out, sib_in,
     gains, gains_in,
-    buf_n, rep_n, gat_n, buf_e, rep_e, gat_e,
+    d_pre_s, buf_n, rep_n, buf_e, rep_e,
     send_sem, recv_sem, nsend, nrecv, esend, erecv, gsend, grecv,
     *level_refs,
 ):
@@ -172,6 +188,15 @@
             device_id=device, device_id_type=MESH,
         )
 
+    pairs = (
+        (h_ef, ef_ref), (h_wei, wei_ref), (h_nf, nf_ref), (h_send, send_ref), (h_recv, recv_ref),
+        (h_weo, weo_ref), (h_ge, ge_ref), (h_wni, wni_ref), (h_wno, wno_ref), (h_gn, gn_ref),
+        (h_dn, dn_ref), (h_de, de_ref),
+    )
+    loads = [pltpu.make_async_copy(a, b, load_sem.at[i]) for i, (a, b) in enumerate(pairs)]
+    for load in loads:
+        load.start()
+
     barrier = pltpu.get_barrier_semaphore()
 
     def greet(device):
@@ -198,20 +223,22 @@
     pl.semaphore_wait(barrier, 1 + level_partners + around)
 
     own = 1 + rep
-    to_sib = remote(nf_ref, ext.at[own], 0, (row, sib))
+    to_sib = remote(h_nf, ext.at[own], 0, (row, sib))
     to_sib.start()
     goes = ((rep == 0) & has_prev) | ((rep == 1) & has_next)
     target = jnp.where(rep == 0, row - 1, row + 1)
     place = jnp.where(rep == 0, 3, 0)
 
     def halo_copy(r):
-        return remote(nf_ref, ext.at[place], 1 + r, (target, r), there=jnp.where(rep == 0, 4, 3))
+        return remote(h_nf, ext.at[place], 1 + r, (target, r), there=jnp.where(rep == 0, 4, 3))
 
     @pl.when(goes)
     def _():
         for r in range(2):
             halo_copy(r).start()
 
+    for load in loads[:5]:
+        load.wait()
     ext[own] = nf_ref[...]
 
     @pl.when(jnp.logical_not(has_prev))
@@ -250,6 +277,8 @@
 
     lax.fori_loop(0, n_chunks, edge_part, 0)
     psum[...] = jnp.zeros_like(psum)
+    for load in loads[5:]:
+        load.wait()
 
     to_sib.wait()
 
@@ -287,7 +316,6 @@
         norm_s[at, :] = norm
         scale_s[at, :] = scale
         message = live_of(c) * norm * gain_e
-        edges_out[at, :] = (ef_ref[at, :].astype(F32) + message).astype(BF16)
         r_row = recv_ref[:, at] - group_start
         sums = mm(row_table(r_row, 2 * shard), message.astype(BF16))
         psum[...] += sums.reshape((2, shard, width))
@@ -303,6 +331,14 @@
     r_sum[...] = jnp.zeros_like(r_sum)
     dwe[...] = jnp.zeros_like(dwe)
     dwo[...] = jnp.zeros_like(dwo)
+
+    def finish_edges(c, carry):
+        at = rows_of(c)
+        message = live_of(c) * norm_s[at, :] * gain_e
+        edges_out[at, :] = (ef_ref[at, :].astype(F32) + message).astype(BF16)
+        return carry
+
+    lax.fori_loop(0, n_chunks, finish_edges, 0)
     agg_copy.wait()
     agg = (psum[rep] + psum_in[...]).astype(BF16)
     node_pre = half_pre + mm(agg, wni_ref[width:, :])
@@ -322,7 +358,7 @@
     big_n[2 * width : 3 * width, :] = contract_rows(node_act, d_mix)
     if big_n.shape[0] > 3 * width:
         big_n[3 * width :, :] = jnp.zeros((big_n.shape[0] - 3 * width, width), F32)
-    red_n.put(big_n, 0)
+    red_n.put(big_n)
     red_n.start_rep()
     nodes_out[...] = (nf.astype(F32) + node_norm * gain_n).astype(BF16)
     gains[0, 1:2, :] = jnp.sum(grad * node_norm, axis=0, keepdims=True)
@@ -349,13 +385,12 @@
         r_row = recv_ref[:, at] - group_start
         s_sum[...] += mm(row_table(s_row, 4 * shard), d_pre)
         r_sum[...] += mm(row_table(r_row, 2 * shard), d_pre)
-        d_edges[at, :] = (d_out + times_transpose(d_pre, wei_ref[:width, :])).astype(BF16)
+        d_pre_s[at, :] = d_pre
         return carry
 
+    red_n.add_rep()
     half = (n_chunks + 1) // 2
     lax.fori_loop(0, half, backward, 0)
-    red_n.add_rep()
-    red_n.start_level(0)
     lax.fori_loop(half, n_chunks, backward, 0)
 
     sends_b = s_sum[...].astype(BF16)
@@ -367,7 +402,7 @@
     big_e[3 * width : 4 * width, :] = dwo[...]
     if big_e.shape[0] > 4 * width:
         big_e[4 * width :, :] = jnp.zeros((big_e.shape[0] - 4 * width, width), F32)
-    red_e.put(big_e, 0)
+    red_e.put(big_e)
     red_e.start_rep()
 
     slot = [0]
@@ -421,16 +456,29 @@
     sib_copy = remote(sib_out.at[sib], sib_in, 11, (row, sib))
     sib_copy.start()
 
+    def stage_of(level):
+        return [(red_e.partner(level, k)[0], rep) for k in range(1, digits[level][1])]
+
     red_n.add_level(0)
+    if levels > 1:
+        red_n.start_level(1)
+    red_e.add_rep()
+    gain_add(going)
+    going = gain_start(stage_of(0))
+
+    def finish_d_edges(c, carry):
+        at = rows_of(c)
+        back = times_transpose(d_pre_s[at, :], wei_ref[:width, :])
+        d_edges[at, :] = (de_ref[at, :].astype(F32) + back).astype(BF16)
+        return carry
+
     for level in range(1, levels):
-        red_n.start_level(level)
-        if level == 1:
-            red_e.add_rep()
-            gain_add(going)
-            red_e.start_level(0)
-            going = gain_start([(red_e.partner(0, k)[0], rep) for k in range(1, digits[0][1])])
         red_n.add_level(level)
-    red_n.start_gather(levels - 1)
+        if level + 1 < levels:
+            red_n.start_level(level + 1)
+    if levels > 1:
+        red_n.start_gather(levels - 1)
+    lax.fori_loop(0, n_chunks, finish_d_edges, 0)
 
     sib_copy.wait()
     total = direct + sib_out[rep] + sib_in[...]
@@ -455,48 +503,58 @@
     def _():
         d_nodes[...] = total.astype(BF16)
 
-    if levels == 1:
-        red_e.add_rep()
-        gain_add(going)
-        red_e.start_level(0)
-        going = gain_start([(red_e.partner(0, k)[0], rep) for k in range(1, digits[0][1])])
-    red_n.wait()
-    if levels > 1:
-        red_n.start_gather(levels - 2)
+    for level in reversed(range(1, levels)):
+        red_n.wait()
+        if level > 1:
+            red_n.start_gather(level - 1)
+    red_n.start_gather_last()
     for level in range(levels):
         red_e.add_level(level)
+        if level + 1 < levels:
+            red_e.start_level(level + 1)
+        elif levels > 1:
+            red_e.start_gather(level)
         gain_add(going)
         if level + 1 < levels:
-            red_e.start_level(level + 1)
-            going = gain_start(
-                [(red_e.partner(level + 1, k)[0], rep) for k in range(1, digits[level + 1][1])]
-            )
-    for level in reversed(range(levels)):
-        red_e.start_gather(level)
-        if level < levels - 1:
-            red_n.wait()
-            if level > 0:
-                red_n.start_gather(level - 1)
-            else:
-                red_n.start_gather_rep()
+            going = gain_start(stage_of(level + 1))
+        if level == 0:
+            red_n.forward()
+    o_gains[...] = gains[levels + 1]
+    for level in reversed(range(1, levels)):
         red_e.wait()
-    if levels == 1:
-        red_n.start_gather_rep()
-    red_e.start_gather_rep()
-    o_ge[...] = gains[levels + 1, 0:1, :]
-    o_gn[...] = gains[levels + 1, 1:2, :]
+        if level > 1:
+            red_e.start_gather(level - 1)
+    red_e.start_gather_last()
     red_n.wait()
+    red_e.forward()
+    red_e.wait()
+
+
+def unpack(*refs):
+    ins, outs, held, load_sem, store_sem = refs[:7], refs[7:17], refs[17:24], refs[24], refs[25]
+    loads = [pltpu.make_async_copy(a, b, load_sem.at[i]) for i, (a, b) in enumerate(zip(ins, held))]
+    for load in loads:
+        load.start()
+    stores = [pltpu.make_async_copy(held[i], outs[i], store_sem.at[i]) for i in range(4)]
+    for load, store in zip(loads, stores):
+        load.wait()
+        store.start()
+    for load in loads[4:]:
+        load.wait()
+    gat_e, gat_n, gains = held[4:]
+    o_wei, o_weo, o_ge, o_wni, o_wno, o_gn = outs[4:]
+    o_ge[...] = gains[0:1, :]
+    o_gn[...] = gains[1:2, :]
     for h in range(2):
         lanes = slice(h * LANES, (h + 1) * LANES)
-        full = red_n.take(h)
-        o_wni[:, lanes] = full[: 2 * width]
-        o_wno[:, lanes] = full[2 * width : 3 * width]
-    red_e.wait()
-    for h in range(2):
-        lanes = slice(h * LANES, (h + 1) * LANES)
-        full = red_e.take(h)
-        o_wei[:, lanes] = full[: 3 * width]
-        o_weo[:, lanes] = full[3 * width : 4 * width]
+        full = gat_e[h].reshape((-1, LANES))
+        o_wei[:, lanes] = full[: o_wei.shape[0]]
+        o_weo[:, lanes] = full[o_wei.shape[0] : o_wei.shape[0] + o_weo.shape[0]]
+        full = gat_n[h].reshape((-1, LANES))
+        o_wni[:, lanes] = full[: o_wni.shape[0]]
+        o_wno[:, lanes] = full[o_wni.shape[0] : o_wni.shape[0] + o_wno.shape[0]]
+    for store in stores:
+        store.wait()
 
 
 def local(
@@ -507,13 +565,14 @@
 ):
     shard, width = node_feats.shape
     edges = edge_feats.shape[0]
-    chunk = min(edges, 256)
+    chunk = min(edges, 512)
     digits = digits_of(n_row)
     radices = tuple(r for _, r in digits)
     partners = sum(r - 1 for r in radices)
+    hbm = pl.BlockSpec(memory_space=pl.ANY)
     vmem, smem = pl.BlockSpec(memory_space=pltpu.VMEM), pl.BlockSpec(memory_space=pltpu.SMEM)
 
-    def reduction(rows):
+    def reduction(rows, radices):
         block = -(-rows // (16 * n_row)) * 16
         tail = (block, LANES)
         levels = [
@@ -521,16 +580,22 @@
         ]
         return (
             block * n_row,
-            [pltpu.VMEM((2,) + radices + tail, BF16), pltpu.VMEM(radices + tail, BF16),
-             pltpu.VMEM((2,) + radices + tail, BF16)],
+            [pltpu.VMEM((2,) + radices + tail, BF16), pltpu.VMEM(radices + tail, BF16)],
             levels,
+            jax.ShapeDtypeStruct((2,) + radices + tail, BF16),
         )
 
-    rows_n, bufs_n, levels_n = reduction(3 * width)
-    rows_e, bufs_e, levels_e = reduction(4 * width)
-    copies = 2 * (1 + partners)
+    rows_n, bufs_n, levels_n, gathered_n = reduction(3 * width, radices)
+    rows_e, bufs_e, levels_e, gathered_e = reduction(4 * width, radices)
+    copies = 2 * (max(radices) + partners)
     dma = pltpu.SemaphoreType.DMA
+    loaded = (
+        node_feats, edge_feats, senders[None, :], receivers[None, :], w_edge_in, w_edge_out,
+        gain_edge[None, :], w_node_in, w_node_out, gain_node[None, :], d_nodes_out, d_edges_out,
+    )
     scratch = [
+        *[pltpu.VMEM(a.shape, a.dtype) for a in loaded],
+        dma((len(loaded),)),
         pltpu.VMEM((4, shard, width), BF16),
         pltpu.VMEM((6 * shard, width), BF16),
         pltpu.VMEM((edges, 8), jnp.int32),
@@ -553,6 +618,7 @@
         pltpu.VMEM((shard, width), F32),
         pltpu.VMEM((len(digits) + 2, 8, width), F32),
         pltpu.VMEM((1 + partners, 8, width), F32),
+        pltpu.VMEM((edges, width), BF16),
         *bufs_n,
         *bufs_e,
         dma((12,)), dma((12,)),
@@ -561,32 +627,38 @@
         *levels_n,
         *levels_e,
     ]
-    out = pl.pallas_call(
+    big = [jax.ShapeDtypeStruct((n, width), BF16) for n in (shard, edges, shard, edges)]
+    held = pl.pallas_call(
         functools.partial(kernel, digits, n_row, chunk),
-        out_shape=(
-            jax.ShapeDtypeStruct((shard, width), BF16),
-            jax.ShapeDtypeStruct((edges, width), BF16),
-            jax.ShapeDtypeStruct((shard, width), BF16),
-            jax.ShapeDtypeStruct((edges, width), BF16),
-            jax.ShapeDtypeStruct(w_edge_in.shape, BF16),
-            jax.ShapeDtypeStruct(w_edge_out.shape, BF16),
-            jax.ShapeDtypeStruct((1, width), F32),
-            jax.ShapeDtypeStruct(w_node_in.shape, BF16),
-            jax.ShapeDtypeStruct(w_node_out.shape, BF16),
-            jax.ShapeDtypeStruct((1, width), F32),
-        ),
-        in_specs=[vmem] * 4 + [smem] + [vmem] * 8,
-        out_specs=tuple([vmem] * 10),
+        out_shape=(*big, gathered_e, gathered_n, jax.ShapeDtypeStruct((8, width), F32)),
+        in_specs=[hbm] * 4 + [smem] + [hbm] * 8,
+        out_specs=tuple([vmem] * 7),
         scratch_shapes=scratch,
         compiler_params=pltpu.CompilerParams(
             collective_id=0, has_side_effects=True, vmem_limit_bytes=60 * 2**20
         ),
         name="layer",
     )(
-        node_feats, edge_feats, senders[None, :], receivers[None, :], edge_count,
-        w_edge_in, w_edge_out, gain_edge[None, :], w_node_in, w_node_out, gain_node[None, :],
-        d_nodes_out, d_edges_out,
-    )
+        *loaded[:4], edge_count, *loaded[4:],
+    )
+    flat = jax.ShapeDtypeStruct((1, width), F32)
+    out = pl.pallas_call(
+        unpack,
+        out_shape=(
+            *big,
+            jax.ShapeDtypeStruct(w_edge_in.shape, BF16),
+            jax.ShapeDtypeStruct(w_edge_out.shape, BF16),
+            flat,
+            jax.ShapeDtypeStruct(w_node_in.shape, BF16),
+            jax.ShapeDtypeStruct(w_node_out.shape, BF16),
+            flat,
+        ),
+        in_specs=[hbm] * 7,
+        out_specs=tuple([hbm] * 4 + [vmem] * 6),
+        scratch_shapes=[pltpu.VMEM(a.shape, a.dtype) for a in held] + [dma((7,)), dma((4,))],
+        compiler_params=pltpu.CompilerParams(vmem_limit_bytes=60 * 2**20),
+        name="unpack",
+    )(*held)
     return (*out[:6], out[6][0], *out[7:9], out[9][0])
 
 

time: 59.3 us -> 48.1 us (0.81)
  local copies, waits for them, and re-layouts: 9.66 us -> 0 us
  Pallas kernels: 48 us -> 46.6 us
    unnamed x26 -> x0, local copies, waits for them, and re-layouts: 9.66 us -> none
    pallas_call x1, Pallas kernels: 48 us -> 43.5 us  [local(): pl.pallas_call(functools.partial(kernel, digits, n_row, chunk), out_shape...]
    pallas_call x0 -> x1, Pallas kernels: none -> 3.09 us  [local(): pl.pallas_call(unpack, out_shape=(*big, jax.ShapeDtypeStruct(w_edge_in.sh...]
where the time goes in v2:
time: 48.1 us; the launch traced here: 47.9 us
  Pallas kernels  46.6 us (97%)
  between operations  1.3 us (3%)
    pallas_call x1, Pallas kernels, local(): pl.pallas_call(functools.partial(kernel, digits, n_row, chunk), out_shape...  43.5 us
    pallas_call x1, Pallas kernels, local(): pl.pallas_call(unpack, out_shape=(*big, jax.ShapeDtypeStruct(w_edge_in.sh...  3.09 us

profile of v2, /device:TPU:0, one launch (start us, length us, event | category | flops | bytes accessed | tf_op | source)
XLA Modules:
  0.0 47.9 jit_solution(12163700350440452805)
XLA Ops:
  1.3 43.5 %layer.1 = (bf16[128,256]{1,0:T(8,128)(2,1)}, bf16[1024,256]{1,0:T(8,128)(2,1)}, bf16[128,256]{1,0:T(8,128)(2,1)}, bf16[1024,256]{1,0:T(8,128)(2,1)}, bf16[2,4,4...) custom-call(bf16[128,256]{1,0:T(8,128)(2,1)} %h_nf.1, bf16[1024,256]{1,0:T(8,128)(2,1)} %h_ef.1, ...), custom_call_target="tpu_custom_call" | custom-call | tf_op jit(solution)/shard_map/layer/pallas_call | solution.py:631
  44.8 3.1 %unpack.1 = (bf16[128,256]{1,0:T(8,128)(2,1)}, bf16[1024,256]{1,0:T(8,128)(2,1)}, bf16[128,256]{1,0:T(8,128)(2,1)}, bf16[1024,256]{1,0:T(8,128)(2,1)}, bf16[768,...) custom-call(bf16[128,256]{1,0:T(8,128)(2,1)} %get-tuple-element.27.r, ...), custom_call_target="tpu_custom_call" | custom-call | tf_op jit(solution)/shard_map/unpack/pallas_call | solution.py:645
